TPU v7x, 32 devices: a whole 2x2x4 slice. The times are simulated.
32 devices in a mesh: grp: 2 (over x), row: 2 (over core), col: 8 (over z, y).
Axes of the slice: x: 2, y: 2, z: 4, core: 2. Of those that a mesh axis runs over, the one named last changes fastest.
Arguments:
- hidden_acts: bfloat16 [512, 26624], P(('grp', 'row'), 'col'), parts along dimension 0, may hold values from -216 to 216
- down_weight: bfloat16 [26624, 8192], P('col', 'row'), may hold values from -0.0390625 to 0.0390625
- amax_history: float32 [8], P('grp'), parts along dimension 0, may hold values from 3 to 12
Outputs:
- scaled_out: bfloat16 [512, 8192], P(('grp', 'col'), 'row'), parts along dimension 0
- token_scale: float32 [512], P(('grp', 'row')), parts along dimension 0
- history_next: float32 [8], P('grp'), parts along dimension 0
There are 2 independent parts, one for each index of `grp`. A program takes and returns all parts, laid end to end along the dimension named above; an argument that names none is the same for every part. Nothing has to cross between parts.
All inputs are finite; a program needn't handle non-finite values.
Results may differ from a plain program's by a relative error of at most 0.0044.
Values may be sent and summed in bfloat16 or wider, within the bound.
No kernel may reach another device: no remote copies, remote signals or barrier semaphores. Data moves between devices by JAX's collectives and lax.ppermute only.
A program may use at most 64 MiB of HBM per device.

v0:
```python
import jax
import jax.numpy as jnp
from jax import lax
from jax.sharding import PartitionSpec as P

clip_ratio = 0.5
format_limit = 448.0


def clip_scaled(values, scales):
    return jnp.clip(
        values.astype(jnp.float32) / scales[:, None], -format_limit, format_limit
    ).astype(jnp.bfloat16)


def on_device(hidden_acts, down_weight, amax_history):
    local_peak = jnp.max(jnp.abs(hidden_acts), axis=1).astype(jnp.float32)
    token_peak = lax.pmax(local_peak, "col")
    own_scale = clip_ratio * (token_peak + 1e-06) / format_limit
    quantized = clip_scaled(hidden_acts, own_scale)
    all_quant = lax.all_gather(quantized, "row", axis=0, tiled=True)
    all_scale = lax.all_gather(own_scale, "row", axis=0, tiled=True)
    previous = jnp.max(amax_history)
    block_rows = all_quant.shape[0] // lax.axis_size("col")
    summed = lax.psum_scatter(
        jnp.dot(all_quant, down_weight, preferred_element_type=jnp.float32),
        "col",
        scatter_dimension=0,
        tiled=True,
    )
    block_scale = lax.dynamic_slice_in_dim(
        all_scale, lax.axis_index("col") * block_rows, block_rows
    )
    result = summed * block_scale[:, None]
    local_max = jnp.max(jnp.abs(result))
    scaled_out = jnp.clip(result / previous, -1.0, 1.0).astype(jnp.bfloat16)
    newest = lax.pmax(local_max, ("row", "col"))
    history_next = jnp.concatenate([newest[None], amax_history[:-1]])
    return (scaled_out, own_scale, history_next)


def solution(mesh):
    in_specs = (P(("grp", "row"), "col"), P("col", "row"), P("grp"))
    out_specs = (P(("grp", "col"), "row"), P(("grp", "row")), P("grp"))
    return jax.shard_map(
        on_device, mesh=mesh, in_specs=in_specs, out_specs=out_specs, check_vma=False
    )
```

profile of v0, /device:TPU:0, one launch (start us, length us, event | category | flops | bytes accessed | tf_op | source)
XLA Modules:
  0.0 189.5 jit_solution(5066335631180745152)
XLA Ops:
  7.2 0.0 all-gather.3.cloned.1.call-start
  7.2 1.4 abs_reduce_fusion
  8.6 23.2 %pmax.14 = f32[128]{0:T(128)S(1)} all-reduce(bf16[128]{0:T(256)(128)(2,1)S(1)} %abs_reduce_fusion), channel_id=1, replica_groups=mesh['grp'=2,'row'=2,'col'=8] {'col'}, use_global_device_ids=true, to_apply=%region_1.0 | all-reduce | flops 128 | bytes 768 | tf_op jit(solution)/shard_map/pmax | solution.py:18
  31.8 0.0 copy-start
  31.8 2.3 %clamp_convert_fusion = bf16[128,3328]{1,0:T(8,128)(2,1)} fusion(bf16[128,3328]{1,0:T(8,128)(2,1)} %param.3, f32[128]{0:T(128)S(1)} %add_multiply_fusion), kind=kLoop, calls=%fused_computation | loop fusion | flops 1703936 | bytes 1704448 | tf_op jit(solution)/shard_map/convert_element_type | solution.py:13
  34.1 0.0 all-gather.3.cloned.1.call-update
  34.1 0.0 reduce-scatter.2.cloned.1.call-start
  34.2 7.4 %all-gather.3.cloned.1.call-done = bf16[256,3328]{1,0:T(8,128)(2,1)} async-done(((bf16[128,3328]{1,0:T(8,128)(2,1)}), bf16[256,3328]{1,0:T(8,128)(2,1)}) %all-gather.3.cloned.1.call-update) | async-done | bytes 1703952 | tf_op jit(solution)/shard_map/all_gather | solution.py:21
  41.5 14.3 %fusion = f32[256,4096]{1,0:T(8,128)} fusion(bf16[256,3328]{1,0:T(8,128)(2,1)} %all-gather.3.cloned.1.call-done, bf16[3328,4096]{1,0:T(8,128)(2,1)} %param.4), kind=kOutput, calls=%fused_computation.6 | convolution fusion | flops 6979321856 | bytes 33161216 | tf_op jit(solution)/shard_map/dot_general | solution.py:26
  55.8 0.0 copy-done
  55.8 0.0 copy-start.1
  55.8 0.0 reduce-scatter.2.cloned.1.call-update
  55.9 1.8 all-gather
  57.7 0.1 dynamic_slice.3
  57.7 0.0 copy-done.1
  57.7 0.6 reduce_max.28
  58.3 87.1 %reduce-scatter.2.cloned.1.call-done = f32[32,4096]{1,0:T(8,128)} async-done(((f32[256,4096]{1,0:T(8,128)}), f32[32,4096]{1,0:T(8,128)}) %reduce-scatter.2.cloned.1.call-update) | async-done | bytes 524304 | tf_op jit(solution)/shard_map/reduce_scatter | solution.py:25
  145.5 3.2 %abs_reduce_fusion.1 = (f32[]{:T(128)}, bf16[32,4096]{1,0:T(8,128)(2,1)}) fusion(f32[32,4096]{1,0:T(8,128)} %reduce-scatter.2.cloned.1.call-done, f32[32]{0:T(128)S(1)} %dynamic_slice.3, f32[]{:T(128)} %reduce_max.28), kind=kLoop, calls=%fused_computation.2 | loop fusion | flops 786431 | bytes 786568 | tf_op jit(solution)/shard_map/reduce_max | solution.py:35
  148.7 32.8 %pmax.15 = f32[1]{0:T(128)} all-reduce(f32[1]{0:T(128)} %bitcast.2), channel_id=1, replica_groups=mesh['grp'=2,'row'=2,'col'=8] {'row','col'}, use_global_device_ids=true, to_apply=%region_5.6 | all-reduce | flops 1 | bytes 8 | tf_op jit(solution)/shard_map/pmax | solution.py:37
  181.5 1.1 pad_maximum_fusion
  (2 shorter events, 0.0 us)
Async XLA Ops:
  7.2 34.4 %all-gather.3.cloned.1.call-start = ((), (), s32[]{:S(2)}) async-start(), calls=%async_computation.1 | async-start | bytes 2555904 | tf_op jit(solution)/shard_map/all_gather | solution.py:21
  31.8 24.0 %copy-start = (f32[128]{0:T(128)}, f32[128]{0:T(128)S(1)}, u32[]{:S(2)}) copy-start(f32[128]{0:T(128)S(1)} %add_multiply_fusion) | copy-start | bytes 1540
  34.1 111.3 %reduce-scatter.2.cloned.1.call-start = ((), (), s32[]{:S(2)}) async-start(), calls=%async_computation.2 | async-start | bytes 4718592 | tf_op jit(solution)/shard_map/reduce_scatter | solution.py:25
  55.8 1.9 %copy-start.1 = (f32[4]{0:T(128)S(1)}, f32[4]{0:T(128)}, u32[]{:S(2)}) copy-start(f32[4]{0:T(128)} %param.5) | copy-start | bytes 52
Sparse Core Ops, SparseCore 0:
  34.2 7.2 all-gather.2
  56.0 89.4 reduce-scatter.1
where the time goes:
time: 190 us; the launch traced here: 189 us
  waiting for transfers between devices  94.5 us (50%)
  blocking collectives  57.8 us (30%)
  matrix products  14.3 us (8%)
  between operations  14.1 us (7%)
  other arithmetic  8.67 us (5%)
    reduce_scatter x1, waiting for transfers between devices, on_device(): lax.psum_scatter(jnp.dot(all_quant, down_weight, preferred_element_type=j...  87.1 us
    pmax x1, blocking collectives, on_device(): newest = lax.pmax(local_max, ('row', 'col'))  32.8 us
    pmax x1, blocking collectives, on_device(): token_peak = lax.pmax(local_peak, 'col')  23.2 us
    dot_general x1, matrix products, on_device(): jnp.dot(all_quant, down_weight, preferred_element_type=jnp.float32)  14.3 us
    all_gather x1, waiting for transfers between devices, on_device(): all_quant = lax.all_gather(quantized, 'row', axis=0, tiled=True)  7.35 us
  transfers between devices with their start and end apart: 2, of which 2 were waited for; matrix products, arithmetic and copies ran while one was open for 0% of the time, Pallas kernels for 0%

commit v1 on v0

--- a/solution.py
+++ b/solution.py
@@ -1,3 +1,4 @@
+import functools
 import jax
 import jax.numpy as jnp
 from jax import lax
@@ -5,6 +6,17 @@
 
 clip_ratio = 0.5
 format_limit = 448.0
+
+
+def try_all_classes(content, join_dim, axis_tag):
+    a_now = jnp.concatenate(
+        jax.lax.all_to_all(jnp.stack([content] * jax.lax.axis_size(axis_tag)), axis_tag, 0, 0),
+        axis=join_dim,
+    )
+    return a_now
+
+
+numbers_run = functools.partial(try_all_classes, join_dim=0, axis_tag="row")
 
 
 def clip_scaled(values, scales):
@@ -18,7 +30,7 @@
     token_peak = lax.pmax(local_peak, "col")
     own_scale = clip_ratio * (token_peak + 1e-06) / format_limit
     quantized = clip_scaled(hidden_acts, own_scale)
-    all_quant = lax.all_gather(quantized, "row", axis=0, tiled=True)
+    all_quant = numbers_run(quantized)
     all_scale = lax.all_gather(own_scale, "row", axis=0, tiled=True)
     previous = jnp.max(amax_history)
     block_rows = all_quant.shape[0] // lax.axis_size("col")

time: 190 us -> 184 us (0.968)
  waiting for transfers between devices: 94.5 us -> 83.2 us
  blocking collectives: 57.8 us -> 62.9 us
    all_gather x1 -> x0, waiting for transfers between devices: 7.35 us -> none  [on_device(): all_quant = lax.all_gather(quantized, 'row', axis=0, tiled=True)]
    all_to_all x0 -> x1, blocking collectives: none -> 5.1 us  [try_all_classes(): jax.lax.all_to_all(jnp.stack([content] * jax.lax.axis_size(axis_tag)), ax...]
    reduce_scatter x1, waiting for transfers between devices: 87.1 us -> 83.2 us  [on_device(): lax.psum_scatter(jnp.dot(all_quant, down_weight, preferred_element_type=j...]
    convert_element_type x1 -> x0, other arithmetic: 2.33 us -> none  [clip_scaled(): return jnp.clip(values.astype(jnp.float32) / scales[:, None], -format_lim...]
  transfers between devices with their start and end apart: 2 -> 1, of which waited for: 2 -> 1; matrix products, arithmetic and copies ran while one was open for 0% -> 0% of each run, Pallas kernels for 0% -> 0%
where the time goes in v1:
time: 184 us; the launch traced here: 183 us
  waiting for transfers between devices  83.2 us (45%)
  blocking collectives  62.9 us (34%)
  matrix products  15.2 us (8%)
  between operations  14.1 us (8%)
  other arithmetic  7.91 us (4%)
    reduce_scatter x1, waiting for transfers between devices, on_device(): lax.psum_scatter(jnp.dot(all_quant, down_weight, preferred_element_type=j...  83.2 us
    pmax x1, blocking collectives, on_device(): newest = lax.pmax(local_max, ('row', 'col'))  32.8 us
    pmax x1, blocking collectives, on_device(): token_peak = lax.pmax(local_peak, 'col')  23.2 us
    dot_general x1, matrix products, on_device(): jnp.dot(all_quant, down_weight, preferred_element_type=jnp.float32)  15.2 us
    all_to_all x1, blocking collectives, try_all_classes(): jax.lax.all_to_all(jnp.stack([content] * jax.lax.axis_size(axis_tag)), ax...  5.1 us
  transfers between devices with their start and end apart: 1, of which 1 were waited for; matrix products, arithmetic and copies ran while one was open for 0% of the time, Pallas kernels for 0%

profile of v1, /device:TPU:0, one launch (start us, length us, event | category | flops | bytes accessed | tf_op | source)
XLA Modules:
  0.0 183.4 jit_solution(12844243246227661822)
XLA Ops:
  7.2 0.0 reduce-scatter.2.cloned.1.call-start
  7.2 1.4 abs_reduce_fusion
  8.6 23.2 %pmax.14 = f32[128]{0:T(128)S(1)} all-reduce(bf16[128]{0:T(256)(128)(2,1)S(1)} %abs_reduce_fusion), channel_id=1, replica_groups=mesh['grp'=2,'row'=2,'col'=8] {'col'}, use_global_device_ids=true, to_apply=%region_1.0 | all-reduce | flops 128 | bytes 768 | tf_op jit(solution)/shard_map/pmax | solution.py:30
  31.8 0.0 copy-start
  31.8 1.4 fusion
  33.2 0.1 pad_maximum_fusion
  33.4 0.0 copy-done
  33.4 5.1 %all_to_all.5 = bf16[2,128,3328]{2,1,0:T(8,128)(2,1)S(1)} all-to-all(bf16[2,128,3328]{2,1,0:T(8,128)(2,1)S(1)} %pad_maximum_fusion), channel_id=1, replica_groups=mesh['grp'=2,'row'=2,'col'=8] {'row'}, dimensions={0} | all-to-all | bytes 3407872 | tf_op jit(solution)/shard_map/all_to_all | solution.py:13
  38.5 15.2 %fusion.1 = f32[256,4096]{1,0:T(8,128)} fusion(bf16[256,3328]{1,0:T(8,128)(2,1)S(1)} %bitcast.10, bf16[3328,4096]{1,0:T(8,128)(2,1)} %param.4), kind=kOutput, calls=%fused_computation.8 | convolution fusion | flops 6979321856 | bytes 33161216 | tf_op jit(solution)/shard_map/dot_general | solution.py:38
  53.7 0.0 copy-start.1
  53.7 0.0 reduce-scatter.2.cloned.1.call-update
  53.7 1.8 all-gather
  55.5 0.1 dynamic_slice.3
  55.6 0.0 copy-done.1
  55.6 0.6 reduce_max.28
  56.2 83.2 %reduce-scatter.2.cloned.1.call-done = f32[32,4096]{1,0:T(8,128)} async-done(((f32[256,4096]{1,0:T(8,128)}), f32[32,4096]{1,0:T(8,128)}) %reduce-scatter.2.cloned.1.call-update) | async-done | bytes 524304 | tf_op jit(solution)/shard_map/reduce_scatter | solution.py:37
  139.4 3.2 %abs_reduce_fusion.1 = (f32[]{:T(128)}, bf16[32,4096]{1,0:T(8,128)(2,1)}) fusion(f32[32,4096]{1,0:T(8,128)} %reduce-scatter.2.cloned.1.call-done, f32[32]{0:T(128)S(1)} %dynamic_slice.3, f32[]{:T(128)} %reduce_max.28), kind=kLoop, calls=%fused_computation.4 | loop fusion | flops 786431 | bytes 786568 | tf_op jit(solution)/shard_map/reduce_max | solution.py:47
  142.6 32.8 %pmax.15 = f32[1]{0:T(128)} all-reduce(f32[1]{0:T(128)} %bitcast.4), channel_id=1, replica_groups=mesh['grp'=2,'row'=2,'col'=8] {'row','col'}, use_global_device_ids=true, to_apply=%region_5.6 | all-reduce | flops 1 | bytes 8 | tf_op jit(solution)/shard_map/pmax | solution.py:49
  175.4 1.1 pad_maximum_fusion.1
  (2 shorter events, 0.0 us)
Async XLA Ops:
  7.2 132.2 %reduce-scatter.2.cloned.1.call-start = ((), (), s32[]{:S(2)}) async-start(), calls=%async_computation.2 | async-start | bytes 4718592 | tf_op jit(solution)/shard_map/reduce_scatter | solution.py:37
  31.8 1.6 copy-start
  53.7 1.9 %copy-start.1 = (f32[4]{0:T(128)S(1)}, f32[4]{0:T(128)}, u32[]{:S(2)}) copy-start(f32[4]{0:T(128)} %param.5) | copy-start | bytes 52
Sparse Core Ops, SparseCore 0:
  53.8 85.5 reduce-scatter.1
